TPU v7x, 512 devices: a whole 4x4x16 slice. The times are simulated.
512 devices in a mesh: blk: 128 (over y, z_lo, x, core), head: 4 (over z_hi).
Axes of the slice: x: 4, y: 4, z: 16 (z_hi: 4, z_lo: 4; z = z_hi * 4 + z_lo), core: 2. Of those that a mesh axis runs over, the one named last changes fastest.
Arguments:
- query_states: bfloat16 [128, 2, 64, 2048], P('blk', None, 'head'), may hold values from -24 to 24
- key_states: bfloat16 [128, 2, 64, 512], P('blk', None, None, 'head'), may hold values from -6 to 6
- value_states: bfloat16 [128, 2, 64, 512], P('blk', None, None, 'head'), may hold values from -6 to 6
- doc_lengths: int32 [3], replicated, may hold values from 1 to 12288, 16384 in all
- page_slot: int32 [128, 2, 4], replicated, may hold values from 0 to 2047, as said below
Outputs:
- attended: bfloat16 [128, 2, 64, 2048], P('blk', None, None, 'head')
- kv_cache: bfloat16 [2048, 4, 16, 256], P('blk', 'head')
Inputs may be any that keep to these rules, and one draw needn't show every extreme that they name: `page_slot`: all entries differ. The busiest owners hold 16 pages, the least busy 4.
All inputs are finite; a program needn't handle non-finite values.
Results may differ from a plain program's by a relative error of at most 0.007.
Values may be sent and summed in bfloat16 or wider, within the bound.
A program may use at most 64 MiB of HBM per device.

v0:
```python
import jax
import jax.numpy as jnp
from jax import lax
from jax.sharding import PartitionSpec as P

PAGE = 16


def per_device(query_states, key_states, value_states, doc_lengths, page_slot):
    q_local = lax.all_to_all(query_states, "head", split_axis=3, concat_axis=2, tiled=True)
    axis_count = lax.axis_size("blk")
    my_index = lax.axis_index("blk")
    block_tok = q_local.shape[2]
    head_dim = key_states.shape[3]
    group_size = q_local.shape[3] // head_dim
    query_rows = q_local.reshape(2 * block_tok, group_size, head_dim)
    offsets = jnp.arange(block_tok, dtype=jnp.int32)
    doc_bounds = jnp.cumsum(doc_lengths)[:-1]
    page_count = block_tok // PAGE
    slot_count = 4 * page_count
    slot_range = jnp.arange(slot_count, dtype=jnp.int32)
    score_scale = head_dim ** (-0.5)

    def group_positions(owner_ids):
        block_starts = jnp.stack([owner_ids, 2 * axis_count - 1 - owner_ids], axis=1) * block_tok
        return (block_starts[:, :, None] + offsets[None, None, :]).reshape(-1)

    def doc_of(positions):
        return jnp.sum((positions[:, None] >= doc_bounds[None, :]).astype(jnp.int32), axis=1)

    q_pos = group_positions(my_index.reshape(1))
    q_doc = doc_of(q_pos)

    def attend_group(attn_state, key_rows, value_rows, allowed):
        running_max, weight_sum, accum = attn_state
        scores = (
            jnp.einsum("qhd,kd->qhk", query_rows, key_rows, preferred_element_type=jnp.float32)
            * score_scale
        )
        masked = jnp.where(allowed[:, None, :], scores, -1e30)
        new_max = jnp.maximum(running_max, jnp.max(masked, axis=2))
        weights = jnp.where(allowed[:, None, :], jnp.exp(masked - new_max[..., None]), 0.0)
        factor = jnp.exp(running_max - new_max)
        weight_sum = weight_sum * factor + jnp.sum(weights, axis=2)
        update = jnp.einsum(
            "qhk,kd->qhd",
            weights.astype(jnp.bfloat16),
            value_rows,
            preferred_element_type=jnp.float32,
        )
        accum = accum * factor[..., None] + update
        return (new_max, weight_sum, accum)

    def visit_group(attn_state, key_group, value_group, owner_ids):
        key_rows = key_group.reshape(-1, head_dim)
        value_rows = value_group.reshape(-1, head_dim)
        k_pos = group_positions(owner_ids)
        allowed = (k_pos[None, :] <= q_pos[:, None]) & (doc_of(k_pos)[None, :] == q_doc[:, None])
        return attend_group(attn_state, key_rows, value_rows, allowed)

    def place_pages(page_store, key_group, value_group, owner_ids):
        page_rows = jnp.concatenate([key_group, value_group], axis=-1).reshape(
            -1, PAGE * 2 * head_dim
        )
        slot_ids = jnp.take(page_slot, owner_ids, axis=0).reshape(-1) - my_index * slot_count
        selector = (slot_range[:, None] == slot_ids[None, :]).astype(jnp.bfloat16)
        return page_store + jnp.dot(selector, page_rows, preferred_element_type=jnp.float32)

    def fold_groups(step_fn, carried, kv_piece):
        key_piece, value_piece = kv_piece
        piece_len = key_piece.shape[0]
        width = 4
        owner_ids = jnp.arange(piece_len, dtype=jnp.int32).reshape(piece_len // width, width)
        key_groups = key_piece.reshape(piece_len // width, width, 2, block_tok, head_dim)
        value_groups = value_piece.reshape(piece_len // width, width, 2, block_tok, head_dim)

        def visit_one(inner_state, entry_tuple):
            key_group, value_group, owners = entry_tuple
            return (step_fn(inner_state, key_group, value_group, owners), None)

        return lax.scan(visit_one, carried, (key_groups, value_groups, owner_ids))[0]

    empty_store = jnp.zeros((slot_count, PAGE * 2 * head_dim), jnp.float32)
    start_state = (
        jnp.full((2 * block_tok, group_size), -1e30, jnp.float32),
        jnp.zeros((2 * block_tok, group_size), jnp.float32),
        jnp.zeros((2 * block_tok, group_size, head_dim), jnp.float32),
    )
    final_state = fold_groups(
        visit_group,
        start_state,
        (
            lax.all_gather(key_states, "blk", axis=0, tiled=True),
            lax.all_gather(value_states, "blk", axis=0, tiled=True),
        ),
    )
    page_store = fold_groups(
        place_pages,
        empty_store,
        (
            lax.all_gather(key_states, "blk", axis=0, tiled=True),
            lax.all_gather(value_states, "blk", axis=0, tiled=True),
        ),
    )
    running_max, weight_sum, accum = final_state
    attended = (
        (accum / weight_sum[..., None])
        .astype(jnp.bfloat16)
        .reshape(1, 2, block_tok, group_size * head_dim)
    )
    kv_cache = page_store.astype(jnp.bfloat16).reshape(slot_count, 1, PAGE, 2 * head_dim)
    return (attended, kv_cache)


def solution(mesh):
    return jax.shard_map(
        per_device,
        mesh=mesh,
        in_specs=(
            P("blk", None, "head", None),
            P("blk", None, None, "head"),
            P("blk", None, None, "head"),
            P(),
            P(),
        ),
        out_specs=(P("blk", None, None, "head"), P("blk", "head", None, None)),
        check_vma=False,
    )
```

profile of v0, /device:TPU:1, one launch (start us, length us, event | category | flops | bytes accessed | tf_op | source)
XLA Modules:
  0.0 593.8 jit_solution(2853987302329961732)
XLA Ops:
  8.6 2.0 copy.26
  10.7 1.7 reshape.326
  12.4 15.6 %all-to-all-start = ((bf16[4,2,8192]{2,1,0:T(2,128)(2,1)}), bf16[4,2,8192]{2,1,0:T(2,128)(2,1)S(1)}, u32[]{:S(2)}, u32[]{:S(2)}) async-start(bf16[4,2,8192]{2,1,0:T(2,128)(2,1)} %reshape.326), calls=%async_computation | async-start | bytes 262144 | tf_op jit(solution)/shard_map/all_to_all | solution.py:10
  30.2 10.6 %all-to-all-done = bf16[4,2,8192]{2,1,0:T(2,128)(2,1)S(1)} async-done(((bf16[4,2,8192]{2,1,0:T(2,128)(2,1)}), bf16[4,2,8192]{2,1,0:T(2,128)(2,1)S(1)}, u32[]{:S(2)}, u32[]{:S(2)}) %all-to-all-start) | async-done | bytes 131104 | tf_op jit(solution)/shard_map/all_to_all | solution.py:10
  42.1 178.9 %all-gather.3.cloned.1.call-done = bf16[128,2,64,128]{3,2,1,0:T(8,128)(2,1)} async-done(((bf16[1,2,64,128]{3,2,1,0:T(8,128)(2,1)}), bf16[128,2,64,128]{3,2,1,0:T(8,128)(2,1)}) %all-gather.3.cloned.1.call-update) | async-done | bytes 4194320 | tf_op jit(solution)/shard_map/all_gather | solution.py:93
  221.1 205.9 %all-gather.5.cloned.1.call-done = bf16[128,2,64,128]{3,2,1,0:T(8,128)(2,1)} async-done(((bf16[1,2,64,128]{3,2,1,0:T(8,128)(2,1)}), bf16[128,2,64,128]{3,2,1,0:T(8,128)(2,1)}) %all-gather.5.cloned.1.call-update) | async-done | bytes 4194320 | tf_op jit(solution)/shard_map/all_gather | solution.py:94
  427.0 88.9 %while.28 = (s32[]{:T(128)}, f32[128,4]{0,1:T(4,128)S(1)}, f32[128,4]{0,1:T(4,128)S(1)}, f32[128,4,128]{2,0,1:T(8,128)S(1)}, s32[32,4]{1,0:T(8,128)S(1)}, /*inde...) while((s32[]{:T(128)}, f32[128,4]{0,1:T(4,128)S(1)}, ...), condition=%wide.region_6.7_spmd.clone, body=%wide.region_2.6_spmd.clone.sunk | while | flops 136976032 | bytes 4899697 | solution.py:81
  427.8 1.0 constant_dynamic-slice_fusion.5
  430.5 1.0 constant_dynamic-slice_fusion.5
  433.3 1.0 constant_dynamic-slice_fusion.5
  436.1 1.0 constant_dynamic-slice_fusion.5
  438.9 1.0 constant_dynamic-slice_fusion.5
  441.7 1.0 constant_dynamic-slice_fusion.5
  444.4 1.0 constant_dynamic-slice_fusion.5
  447.2 1.0 constant_dynamic-slice_fusion.5
  450.0 1.0 constant_dynamic-slice_fusion.5
  452.8 1.0 constant_dynamic-slice_fusion.5
  455.6 1.0 constant_dynamic-slice_fusion.5
  458.3 1.0 constant_dynamic-slice_fusion.5
  461.1 1.0 constant_dynamic-slice_fusion.5
  463.9 1.0 constant_dynamic-slice_fusion.5
  466.7 1.0 constant_dynamic-slice_fusion.5
  469.4 1.0 constant_dynamic-slice_fusion.5
  472.2 1.0 constant_dynamic-slice_fusion.5
  475.0 1.0 constant_dynamic-slice_fusion.5
  477.8 1.0 constant_dynamic-slice_fusion.5
  480.6 1.0 constant_dynamic-slice_fusion.5
  483.3 1.0 constant_dynamic-slice_fusion.5
  486.1 1.0 constant_dynamic-slice_fusion.5
  488.9 1.0 constant_dynamic-slice_fusion.5
  491.7 1.0 constant_dynamic-slice_fusion.5
  494.5 1.0 constant_dynamic-slice_fusion.5
  497.2 1.0 constant_dynamic-slice_fusion.5
  500.0 1.0 constant_dynamic-slice_fusion.5
  502.8 1.0 constant_dynamic-slice_fusion.5
  505.6 1.0 constant_dynamic-slice_fusion.5
  508.4 1.0 constant_dynamic-slice_fusion.5
  511.1 1.0 constant_dynamic-slice_fusion.5
  513.9 1.0 constant_dynamic-slice_fusion.5
  516.9 69.3 %while.29 = (s32[]{:T(128)}, f32[16,4096]{1,0:T(8,128)S(1)}, s32[32,4]{1,0:T(8,128)S(1)}, s32[128,2,4]{2,1,0:T(2,128)S(1)}, s32[]{:T(128)}, /*index=5*/bf16[32,4...) while((s32[]{:T(128)}, f32[16,4096]{1,0:T(8,128)S(1)}, ...), condition=%wide.region_8.9_spmd.clone, body=%wide.region_7.8_spmd.clone.sunk | while | flops 4851303 | bytes 2364495 | solution.py:81
  519.1 1.0 dynamic-slice_bitcast_fusion.3
  521.2 1.0 dynamic-slice_bitcast_fusion.3
  523.4 1.0 dynamic-slice_bitcast_fusion.3
  525.6 1.0 dynamic-slice_bitcast_fusion.3
  527.7 1.0 dynamic-slice_bitcast_fusion.3
  529.9 1.0 dynamic-slice_bitcast_fusion.3
  532.1 1.0 dynamic-slice_bitcast_fusion.3
  534.2 1.0 dynamic-slice_bitcast_fusion.3
  536.4 1.0 dynamic-slice_bitcast_fusion.3
  538.6 1.0 dynamic-slice_bitcast_fusion.3
  540.7 1.0 dynamic-slice_bitcast_fusion.3
  542.9 1.0 dynamic-slice_bitcast_fusion.3
  545.1 1.0 dynamic-slice_bitcast_fusion.3
  547.2 1.0 dynamic-slice_bitcast_fusion.3
  549.4 1.0 dynamic-slice_bitcast_fusion.3
  551.6 1.0 dynamic-slice_bitcast_fusion.3
  553.7 1.0 dynamic-slice_bitcast_fusion.3
  555.9 1.0 dynamic-slice_bitcast_fusion.3
  558.1 1.0 dynamic-slice_bitcast_fusion.3
  560.2 1.0 dynamic-slice_bitcast_fusion.3
  564.6 1.0 dynamic-slice_bitcast_fusion.3
  571.1 1.0 dynamic-slice_bitcast_fusion.3
  575.4 1.0 dynamic-slice_bitcast_fusion.3
  581.9 1.0 dynamic-slice_bitcast_fusion.3
  (804 shorter events, 104.8 us)
Async XLA Ops:
  7.2 213.9 %all-gather.3.cloned.1.call-start = ((), (), s32[]{:S(2)}) async-start(), calls=%async_computation.1 | async-start | bytes 4227072 | tf_op jit(solution)/shard_map/all_gather | solution.py:93
  7.9 419.1 %all-gather.5.cloned.1.call-start = ((), (), s32[]{:S(2)}) async-start(), calls=%async_computation.2 | async-start | bytes 4227072 | tf_op jit(solution)/shard_map/all_gather | solution.py:94
  12.4 28.3 %all-to-all-start = ((bf16[4,2,8192]{2,1,0:T(2,128)(2,1)}), bf16[4,2,8192]{2,1,0:T(2,128)(2,1)S(1)}, u32[]{:S(2)}, u32[]{:S(2)}) async-start(bf16[4,2,8192]{2,1,0:T(2,128)(2,1)} %reshape.326), calls=%async_computation | async-start | bytes 262144 | tf_op jit(solution)/shard_map/all_to_all | solution.py:10
Sparse Core Ops, SparseCore 0:
  10.2 210.8 all-gather.2
  223.2 203.7 all-gather.4
where the time goes:
time: 595 us; the launch traced here: 594 us
  waiting for transfers between devices  397 us (67%)
  local copies, waits for them, and re-layouts  105 us (18%)
  matrix products  30.2 us (5%)
  other arithmetic  27.7 us (5%)
  starting transfers between devices  15.7 us (3%)
  between operations  14.1 us (2%)
    all_gather x1, waiting for transfers between devices, per_device(): lax.all_gather(value_states, 'blk', axis=0, tiled=True)  206 us
    all_gather x1, waiting for transfers between devices, per_device(): lax.all_gather(key_states, 'blk', axis=0, tiled=True)  179 us
    dynamic_slice x32, local copies, waits for them, and re-layouts, fold_groups(): lax.scan(visit_one, carried, (key_groups, value_groups, owner_ids))[0]  31.8 us
    squeeze x32, local copies, waits for them, and re-layouts, fold_groups(): lax.scan(visit_one, carried, (key_groups, value_groups, owner_ids))[0]  31.7 us
    gather x32, local copies, waits for them, and re-layouts, place_pages(): jnp.take(page_slot, owner_ids, axis=0).reshape(-1) - my_index * slot_count  18.3 us
    all_to_all x1, starting transfers between devices, per_device(): lax.all_to_all(query_states, 'head', split_axis=3, concat_axis=2, tiled=T...  15.6 us
    dot_general x32, matrix products, attend_group(): jnp.einsum('qhk,kd->qhd', weights.astype(jnp.bfloat16), value_rows, prefe...  14.1 us
  transfers between devices with their start and end apart: 3, of which 3 were waited for; matrix products, arithmetic and copies ran while one was open for 1% of the time, Pallas kernels for 0%

commit v1 on v0

--- a/solution.py
+++ b/solution.py
@@ -91,7 +91,10 @@
         start_state,
         (
             lax.all_gather(key_states, "blk", axis=0, tiled=True),
-            lax.all_gather(value_states, "blk", axis=0, tiled=True),
+            jnp.concatenate(
+                lax.all_to_all(jnp.stack([value_states] * lax.axis_size("blk")), "blk", 0, 0),
+                axis=0,
+            ),
         ),
     )
     page_store = fold_groups(

time: 595 us -> 620 us (1.042)
  starting transfers between devices: 15.7 us -> 28.5 us
  waiting for transfers between devices: 397 us -> 405 us
    all_to_all x0 -> x1, starting transfers between devices: none -> 12.8 us  [per_device(): lax.all_to_all(jnp.stack([value_states] * lax.axis_size('blk')), 'blk', 0...]
    all_gather x1, waiting for transfers between devices: 179 us -> 186 us  [per_device(): lax.all_gather(key_states, 'blk', axis=0, tiled=True)]
  transfers between devices with their start and end apart: 3 -> 4, of which waited for: 3 -> 3; matrix products, arithmetic and copies ran while one was open for 1% -> 13% of each run, Pallas kernels for 0% -> 0%
where the time goes in v1:
time: 620 us; the launch traced here: 618 us
  waiting for transfers between devices  405 us (65%)
  local copies, waits for them, and re-layouts  108 us (17%)
  matrix products  30.5 us (5%)
  starting transfers between devices  28.5 us (5%)
  other arithmetic  27.7 us (4%)
  between operations  14.2 us (2%)
    all_gather x1, waiting for transfers between devices, per_device(): lax.all_gather(value_states, 'blk', axis=0, tiled=True)  206 us
    all_gather x1, waiting for transfers between devices, per_device(): lax.all_gather(key_states, 'blk', axis=0, tiled=True)  186 us
    dynamic_slice x32, local copies, waits for them, and re-layouts, fold_groups(): lax.scan(visit_one, carried, (key_groups, value_groups, owner_ids))[0]  31.8 us
    squeeze x32, local copies, waits for them, and re-layouts, fold_groups(): lax.scan(visit_one, carried, (key_groups, value_groups, owner_ids))[0]  31.7 us
    gather x32, local copies, waits for them, and re-layouts, place_pages(): jnp.take(page_slot, owner_ids, axis=0).reshape(-1) - my_index * slot_count  18.3 us
    all_to_all x1, starting transfers between devices, per_device(): lax.all_to_all(query_states, 'head', split_axis=3, concat_axis=2, tiled=T...  15.6 us
    dot_general x32, matrix products, attend_group(): jnp.einsum('qhk,kd->qhd', weights.astype(jnp.bfloat16), value_rows, prefe...  14.5 us
    all_to_all x1, starting transfers between devices, per_device(): lax.all_to_all(jnp.stack([value_states] * lax.axis_size('blk')), 'blk', 0...  12.8 us
  transfers between devices with their start and end apart: 4, of which 3 were waited for; matrix products, arithmetic and copies ran while one was open for 13% of the time, Pallas kernels for 0%

profile of v1, /device:TPU:1, one launch (start us, length us, event | category | flops | bytes accessed | tf_op | source)
XLA Modules:
  0.0 618.4 jit_solution(6852762639450905380)
XLA Ops:
  8.6 2.0 copy.26
  10.7 1.7 reshape.328
  12.4 15.6 %all-to-all-start = ((bf16[4,2,8192]{2,1,0:T(2,128)(2,1)}), bf16[4,2,8192]{2,1,0:T(2,128)(2,1)S(1)}, u32[]{:S(2)}, u32[]{:S(2)}) async-start(bf16[4,2,8192]{2,1,0:T(2,128)(2,1)} %reshape.328), calls=%async_computation | async-start | bytes 262144 | tf_op jit(solution)/shard_map/all_to_all | solution.py:10
  30.2 10.6 %all-to-all-done = bf16[4,2,8192]{2,1,0:T(2,128)(2,1)S(1)} async-done(((bf16[4,2,8192]{2,1,0:T(2,128)(2,1)}), bf16[4,2,8192]{2,1,0:T(2,128)(2,1)S(1)}, u32[]{:S(2)}, u32[]{:S(2)}) %all-to-all-start) | async-done | bytes 131104 | tf_op jit(solution)/shard_map/all_to_all | solution.py:10
  40.7 3.8 stack.12
  44.5 12.8 %all-to-all-start.1 = ((bf16[128,1,2,64,128]{4,3,2,1,0:T(8,128)(2,1)}), bf16[128,1,2,64,128]{4,3,2,1,0:T(8,128)(2,1)}, u32[]{:S(2)}, u32[]{:S(2)}) async-start(bf16[128,1,2,64,128]{4,3,2,1,0:T(8,128)(2,1)} %stack.12), calls=%async_computation.1 | async-start | bytes 8388608 | tf_op jit(solution)/shard_map/all_to_all | solution.py:95
  58.7 186.4 %all-gather.3.cloned.1.call-done = bf16[128,2,64,128]{3,2,1,0:T(8,128)(2,1)} async-done(((bf16[1,2,64,128]{3,2,1,0:T(8,128)(2,1)}), bf16[128,2,64,128]{3,2,1,0:T(8,128)(2,1)}) %all-gather.3.cloned.1.call-update) | async-done | bytes 4194320 | tf_op jit(solution)/shard_map/all_gather | solution.py:93
  245.1 206.2 %all-gather.5.cloned.1.call-done = bf16[128,2,64,128]{3,2,1,0:T(8,128)(2,1)} async-done(((bf16[1,2,64,128]{3,2,1,0:T(8,128)(2,1)}), bf16[128,2,64,128]{3,2,1,0:T(8,128)(2,1)}) %all-gather.5.cloned.1.call-update) | async-done | bytes 4194320 | tf_op jit(solution)/shard_map/all_gather | solution.py:105
  451.4 69.3 %while.29 = (s32[]{:T(128)}, f32[16,4096]{1,0:T(8,128)S(1)}, s32[32,4]{1,0:T(8,128)S(1)}, s32[128,2,4]{2,1,0:T(2,128)S(1)}, s32[]{:T(128)}, /*index=5*/bf16[32,4...) while((s32[]{:T(128)}, f32[16,4096]{1,0:T(8,128)S(1)}, ...), condition=%wide.region_8.9_spmd.clone, body=%wide.region_7.8_spmd.clone.sunk | while | flops 4851303 | bytes 2364495 | solution.py:81
  453.5 1.0 dynamic-slice_bitcast_fusion.3
  455.7 1.0 dynamic-slice_bitcast_fusion.3
  457.9 1.0 dynamic-slice_bitcast_fusion.3
  460.0 1.0 dynamic-slice_bitcast_fusion.3
  462.2 1.0 dynamic-slice_bitcast_fusion.3
  464.4 1.0 dynamic-slice_bitcast_fusion.3
  466.5 1.0 dynamic-slice_bitcast_fusion.3
  468.7 1.0 dynamic-slice_bitcast_fusion.3
  470.9 1.0 dynamic-slice_bitcast_fusion.3
  473.0 1.0 dynamic-slice_bitcast_fusion.3
  475.2 1.0 dynamic-slice_bitcast_fusion.3
  477.4 1.0 dynamic-slice_bitcast_fusion.3
  479.5 1.0 dynamic-slice_bitcast_fusion.3
  481.7 1.0 dynamic-slice_bitcast_fusion.3
  483.9 1.0 dynamic-slice_bitcast_fusion.3
  486.0 1.0 dynamic-slice_bitcast_fusion.3
  488.2 1.0 dynamic-slice_bitcast_fusion.3
  494.7 1.0 dynamic-slice_bitcast_fusion.3
  499.0 1.0 dynamic-slice_bitcast_fusion.3
  505.5 1.0 dynamic-slice_bitcast_fusion.3
  509.8 1.0 dynamic-slice_bitcast_fusion.3
  516.3 1.0 dynamic-slice_bitcast_fusion.3
  521.4 89.2 %while.28 = (s32[]{:T(128)}, f32[128,4]{0,1:T(4,128)S(1)}, f32[128,4]{0,1:T(4,128)S(1)}, f32[128,4,128]{2,0,1:T(8,128)S(1)}, s32[32,4]{1,0:T(8,128)S(1)}, /*inde...) while((s32[]{:T(128)}, f32[128,4]{0,1:T(4,128)S(1)}, ...), condition=%wide.region_6.7_spmd.clone, body=%wide.region_2.6_spmd.clone.sunk | while | flops 136976032 | bytes 4899697 | solution.py:81
  522.1 1.0 constant_dynamic-slice_fusion.5
  524.9 1.0 constant_dynamic-slice_fusion.5
  527.7 1.0 constant_dynamic-slice_fusion.5
  530.5 1.0 constant_dynamic-slice_fusion.5
  533.3 1.0 constant_dynamic-slice_fusion.5
  536.0 1.0 constant_dynamic-slice_fusion.5
  538.8 1.0 constant_dynamic-slice_fusion.5
  541.6 1.0 constant_dynamic-slice_fusion.5
  544.4 1.0 constant_dynamic-slice_fusion.5
  547.2 1.0 constant_dynamic-slice_fusion.5
  550.0 1.0 constant_dynamic-slice_fusion.5
  552.8 1.0 constant_dynamic-slice_fusion.5
  555.6 1.0 constant_dynamic-slice_fusion.5
  558.3 1.0 constant_dynamic-slice_fusion.5
  561.1 1.0 constant_dynamic-slice_fusion.5
  563.9 1.0 constant_dynamic-slice_fusion.5
  566.7 1.0 constant_dynamic-slice_fusion.5
  569.5 1.0 constant_dynamic-slice_fusion.5
  572.3 1.0 constant_dynamic-slice_fusion.5
  575.1 1.0 constant_dynamic-slice_fusion.5
  577.9 1.0 constant_dynamic-slice_fusion.5
  580.6 1.0 constant_dynamic-slice_fusion.5
  583.4 1.0 constant_dynamic-slice_fusion.5
  586.2 1.0 constant_dynamic-slice_fusion.5
  589.0 1.0 constant_dynamic-slice_fusion.5
  591.8 1.0 constant_dynamic-slice_fusion.5
  594.6 1.0 constant_dynamic-slice_fusion.5
  597.4 1.0 constant_dynamic-slice_fusion.5
  600.2 1.0 constant_dynamic-slice_fusion.5
  602.9 1.0 constant_dynamic-slice_fusion.5
  605.7 1.0 constant_dynamic-slice_fusion.5
  608.5 1.0 constant_dynamic-slice_fusion.5
  (807 shorter events, 107.0 us)
Async XLA Ops:
  7.2 238.0 %all-gather.3.cloned.1.call-start = ((), (), s32[]{:S(2)}) async-start(), calls=%async_computation.2 | async-start | bytes 4227072 | tf_op jit(solution)/shard_map/all_gather | solution.py:93
  7.9 443.5 %all-gather.5.cloned.1.call-start = ((), (), s32[]{:S(2)}) async-start(), calls=%async_computation.3 | async-start | bytes 4227072 | tf_op jit(solution)/shard_map/all_gather | solution.py:105
  12.4 28.3 %all-to-all-start = ((bf16[4,2,8192]{2,1,0:T(2,128)(2,1)}), bf16[4,2,8192]{2,1,0:T(2,128)(2,1)S(1)}, u32[]{:S(2)}, u32[]{:S(2)}) async-start(bf16[4,2,8192]{2,1,0:T(2,128)(2,1)} %reshape.328), calls=%async_computation | async-start | bytes 262144 | tf_op jit(solution)/shard_map/all_to_all | solution.py:10
  44.5 476.9 %all-to-all-start.1 = ((bf16[128,1,2,64,128]{4,3,2,1,0:T(8,128)(2,1)}), bf16[128,1,2,64,128]{4,3,2,1,0:T(8,128)(2,1)}, u32[]{:S(2)}, u32[]{:S(2)}) async-start(bf16[128,1,2,64,128]{4,3,2,1,0:T(8,128)(2,1)} %stack.12), calls=%async_computation.1 | async-start | bytes 8388608 | tf_op jit(solution)/shard_map/all_to_all | solution.py:95
Sparse Core Ops, SparseCore 0:
  10.2 234.9 all-gather.2
  247.3 204.0 all-gather.4
